TPU v7x, 32 devices: a whole 2x2x4 slice. The times are simulated.
32 devices in a mesh: rows: 16 (over z, y, x), panel: 2 (over core).
Axes of the slice: x: 2, y: 2, z: 4, core: 2. Of those that a mesh axis runs over, the one named last changes fastest.
Arguments:
- adj_tiles: bfloat16 [16, 2, 2, 16, 128, 128], P('rows', 'panel'), may hold values from -0.25 to 0.25
- row_counts: int32 [16, 2, 2], P('rows', 'panel'), may hold values from 1 to 16, as said below
- tile_cols: int32 [16, 2, 2, 16], P('rows', 'panel'), may hold values from 0 to 15, as said below
- start_basis: bfloat16 [64, 4096], P(None, ('rows', 'panel')), may hold values from -100 to 100
- start_resid: bfloat16 [64, 4096], P(None, ('rows', 'panel')), may hold values from -100 to 100
- start_search: bfloat16 [64, 4096], P(None, ('rows', 'panel')), may hold values from -100 to 100
- ritz_basis: float32 [3, 64, 192], replicated, may hold values from -1 to 1.5
- ritz_search: float32 [3, 64, 128], replicated, may hold values from -1 to 1.5
Outputs:
- eigvectors: float32 [64, 4096], P(None, ('rows', 'panel'))
- residual: float32 [64, 4096], P(None, ('rows', 'panel'))
- directions: float32 [64, 4096], P(None, ('rows', 'panel'))
- rayleigh: float32 [64, 64], replicated
Inputs may be any that keep to these rules, and one draw needn't show every extreme that they name: `row_counts`: each device's row blocks have 1 to 16 live slots, the live ones first; on one device every row block has 16. `tile_cols`: the live slots of one row block name distinct column blocks.
All inputs are finite; a program needn't handle non-finite values.
Results may differ from a plain program's by a relative error of at most 0.0053.
Values may be sent and summed in bfloat16 or wider, within the bound.
No kernel may reach another device: no remote copies, remote signals or barrier semaphores. Data moves between devices by JAX's collectives and lax.ppermute only.
A program may use at most 64 MiB of HBM per device.

v0:
```python
import jax
import jax.numpy as jnp
from jax import lax
from jax.sharding import PartitionSpec as P

epsilon = 1e-06
highest = lax.Precision.HIGHEST


def lower_solve(factor, values):
    return jax.scipy.linalg.solve_triangular(factor, values, lower=True)


def slot_product(gathered, tile_set, counts, columns):
    vec_rows = gathered.shape[0]
    tile_edge = tile_set.shape[2]
    blocks = gathered.reshape(vec_rows, gathered.shape[1] // tile_edge, tile_edge)
    slot_ids = jnp.arange(tile_set.shape[1], dtype=jnp.int32)
    in_use = slot_ids[None, :] < counts[:, None]
    chosen = jnp.take(blocks, columns.reshape(-1), axis=1)
    chosen = chosen.reshape(vec_rows, columns.shape[0], columns.shape[1], tile_edge)
    chosen = jnp.where(in_use[None, :, :, None], chosen, jnp.zeros((), chosen.dtype))
    summed = jnp.einsum("wbjk,bjik->wbi", chosen, tile_set, preferred_element_type=jnp.float32)
    return summed.reshape(vec_rows, -1)


def body(
    adj_tiles,
    row_counts,
    tile_cols,
    start_basis,
    start_resid,
    start_search,
    ritz_basis,
    ritz_search,
):
    tile_set = adj_tiles[0, 0]
    counts = row_counts[0, 0]
    columns = tile_cols[0, 0]
    vec_count = start_basis.shape[0]
    node_total = start_basis.shape[1] * lax.axis_size("rows") * lax.axis_size("panel")
    basis_b, resid_b, search_b = (start_basis, start_resid, start_search)
    for sweep in range(ritz_basis.shape[0]):
        stacked = jnp.concatenate([basis_b, resid_b, search_b], axis=0)
        stacked_all = lax.all_gather(stacked, "rows", axis=1, tiled=True)
        partial_value = slot_product(stacked_all, tile_set, counts, columns)
        product_rows = lax.psum_scatter(partial_value, "panel", scatter_dimension=1, tiled=True)
        stack_f32 = stacked.astype(jnp.float32)
        image_f32 = stack_f32 - product_rows
        mixing = ritz_basis[sweep]
        search_mix = ritz_search[sweep]
        rotated = jnp.dot(mixing, stack_f32, precision=highest)
        rotated_image = jnp.dot(mixing, image_f32, precision=highest)
        search_raw = jnp.dot(search_mix, stack_f32[vec_count:], precision=highest)
        gram_sum, curve_sum, search_sum = lax.psum(
            (
                jnp.dot(rotated, rotated.T, precision=highest),
                jnp.dot(rotated, rotated_image.T, precision=highest),
                jnp.sum(search_raw * search_raw, axis=1),
            ),
            ("rows", "panel"),
        )
        factor = jnp.linalg.cholesky(gram_sum / node_total)
        basis = lower_solve(factor, rotated)
        basis_image = lower_solve(factor, rotated_image)
        rayleigh = lower_solve(factor, lower_solve(factor, curve_sum / node_total).T).T
        resid_raw = basis_image - jnp.dot(rayleigh.T, basis, precision=highest)
        search_sq = search_sum / node_total
        resid_sq = lax.psum(jnp.sum(resid_raw * resid_raw, axis=1), ("rows", "panel")) / node_total
        resid = resid_raw / jnp.sqrt(resid_sq + epsilon)[:, None]
        search = search_raw / jnp.sqrt(search_sq + epsilon)[:, None]
        basis_b = basis.astype(jnp.bfloat16)
        resid_b = resid.astype(jnp.bfloat16)
        search_b = search.astype(jnp.bfloat16)
    return (basis, resid, search, rayleigh)


def solution(mesh):
    return jax.shard_map(
        body,
        mesh=mesh,
        in_specs=(
            P("rows", "panel", None, None, None, None),
            P("rows", "panel", None),
            P("rows", "panel", None, None),
            P(None, ("rows", "panel")),
            P(None, ("rows", "panel")),
            P(None, ("rows", "panel")),
            P(),
            P(),
        ),
        out_specs=(
            P(None, ("rows", "panel")),
            P(None, ("rows", "panel")),
            P(None, ("rows", "panel")),
            P(),
        ),
        check_vma=False,
    )
```

profile of v0, /device:TPU:0, one launch (start us, length us, event | category | flops | bytes accessed | tf_op | source)
XLA Modules:
  0.0 463.8 jit_solution(4816201861021060135)
XLA Ops:
  7.2 0.8 reshape_squeeze.2
  8.1 0.7 constant_dynamic-update-slice_fusion.2
  8.8 0.7 constant_dynamic-update-slice_fusion.1
  9.5 0.7 constant_dynamic-update-slice_fusion
  10.3 47.0 %all_gather.9 = bf16[192,2048]{1,0:T(8,128)(2,1)S(1)} all-gather(bf16[192,128]{1,0:T(8,128)(2,1)S(1)} %constant_dynamic-update-slice_fusion), channel_id=1, replica_groups=mesh['rows'=16,'panel'=2] {'rows'}, dimensions={1}, use_global_device_ids=true | all-gather | bytes 835584 | tf_op jit(solution)/shard_map/all_gather | solution.py:45
  57.6 0.8 gather_fusion
  60.3 1.0 multiply_reduce_fusion.4
  61.5 2.1 reduce-scatter.4.cloned.1.call-done
  63.6 1.1 fusion.30
  64.9 41.0 %all-reduce.5 = (f32[64,64]{0,1:T(8,128)S(1)}, f32[64,64]{0,1:T(8,128)S(1)}) all-reduce(f32[64,64]{0,1:T(8,128)S(1)} %fusion.122, f32[64,64]{0,1:T(8,128)S(1)} %fusion.123), channel_id=1, replica_groups=mesh['rows'=16,'panel'=2] {'rows','panel'}, use_global_device_ids=true, to_apply=%region_0.1 | all-reduce | flops 8192 | bytes 65536 | tf_op jit(solution)/shard_map/psum | solution.py:55
  106.1 5.8 %cholesky.59 = f32[64,64]{1,0:T(8,128)S(1)} custom-call(f32[64,64]{1,0:T(8,128)S(1)} %fusion.95), custom_call_target="Cholesky" | custom-call | tf_op jit(solution)/shard_map/jit(cholesky)/cholesky | solution.py:63
  113.3 4.9 %custom-call.18 = f32[1,64,64]{1,2,0:T(8,128)S(1)} custom-call(f32[1,64,64]{2,1,0:T(8,128)S(1)} %fusion.48), custom_call_target="InvertDiagBlocksLowerTriangular" | custom-call | tf_op jit(solution)/shard_map/jit(_solve_triangular)/triangular_solve | solution.py:11
  119.4 40.0 %all-reduce.4 = (f32[64]{0:T(128)S(1)}, f32[64]{0:T(128)S(1)}) all-reduce(f32[64]{0:T(128)S(1)} %get-tuple-element.32, f32[64]{0:T(128)S(1)} %get-tuple-element.34), channel_id=1, replica_groups=mesh['rows'=16,'panel'=2] {'rows','panel'}, use_global_device_ids=true, to_apply=%region_8.13 | all-reduce | flops 128 | bytes 1024 | tf_op jit(solution)/shard_map/psum | solution.py:55
  159.9 45.3 %all_gather.10 = bf16[192,2048]{1,0:T(8,128)(2,1)S(1)} all-gather(bf16[192,128]{1,0:T(8,128)(2,1)S(1)} %pad_maximum_fusion), channel_id=1, replica_groups=mesh['rows'=16,'panel'=2] {'rows'}, dimensions={1}, use_global_device_ids=true | all-gather | bytes 835584 | tf_op jit(solution)/shard_map/all_gather | solution.py:45
  205.3 0.9 gather_fusion.1
  207.8 1.0 multiply_reduce_fusion.2
  209.0 2.3 reduce-scatter.6.cloned.1.call-done
  211.3 1.1 fusion.27
  212.7 41.0 %all-reduce.3 = (f32[64,64]{0,1:T(8,128)S(1)}, f32[64,64]{0,1:T(8,128)S(1)}) all-reduce(f32[64,64]{0,1:T(8,128)S(1)} %fusion.124, f32[64,64]{0,1:T(8,128)S(1)} %fusion.125), channel_id=1, replica_groups=mesh['rows'=16,'panel'=2] {'rows','panel'}, use_global_device_ids=true, to_apply=%region_9.14 | all-reduce | flops 8192 | bytes 65536 | tf_op jit(solution)/shard_map/psum | solution.py:55
  253.8 5.8 %cholesky.70 = f32[64,64]{1,0:T(8,128)S(1)} custom-call(f32[64,64]{1,0:T(8,128)S(1)} %fusion.84), custom_call_target="Cholesky" | custom-call | tf_op jit(solution)/shard_map/jit(cholesky)/cholesky | solution.py:63
  261.0 4.9 %custom-call.22 = f32[1,64,64]{1,2,0:T(8,128)S(1)} custom-call(f32[1,64,64]{2,1,0:T(8,128)S(1)} %fusion.49), custom_call_target="InvertDiagBlocksLowerTriangular" | custom-call | tf_op jit(solution)/shard_map/jit(_solve_triangular)/triangular_solve | solution.py:11
  267.1 40.1 %all-reduce.2 = (f32[64]{0:T(128)S(1)}, f32[64]{0:T(128)S(1)}) all-reduce(f32[64]{0:T(128)S(1)} %get-tuple-element.36, f32[64]{0:T(128)S(1)} %get-tuple-element.40), channel_id=1, replica_groups=mesh['rows'=16,'panel'=2] {'rows','panel'}, use_global_device_ids=true, to_apply=%region_15.20 | all-reduce | flops 128 | bytes 1024 | tf_op jit(solution)/shard_map/psum | solution.py:55
  307.6 45.4 %all_gather.11 = bf16[192,2048]{1,0:T(8,128)(2,1)S(1)} all-gather(bf16[192,128]{1,0:T(8,128)(2,1)S(1)} %pad_maximum_fusion.1), channel_id=1, replica_groups=mesh['rows'=16,'panel'=2] {'rows'}, dimensions={1}, use_global_device_ids=true | all-gather | bytes 835584 | tf_op jit(solution)/shard_map/all_gather | solution.py:45
  353.3 0.9 gather_fusion.2
  355.7 1.0 multiply_reduce_fusion
  356.9 2.4 reduce-scatter.8.cloned.1.call-done
  359.3 1.1 fusion.24
  360.6 41.0 %all-reduce.1 = (f32[64,64]{0,1:T(8,128)S(1)}, f32[64,64]{0,1:T(8,128)S(1)}) all-reduce(f32[64,64]{0,1:T(8,128)S(1)} %fusion.126, f32[64,64]{0,1:T(8,128)S(1)} %fusion.127), channel_id=1, replica_groups=mesh['rows'=16,'panel'=2] {'rows','panel'}, use_global_device_ids=true, to_apply=%region_16.21 | all-reduce | flops 8192 | bytes 65536 | tf_op jit(solution)/shard_map/psum | solution.py:55
  401.7 5.8 %cholesky.81 = f32[64,64]{1,0:T(8,128)S(1)} custom-call(f32[64,64]{1,0:T(8,128)S(1)} %fusion.73), custom_call_target="Cholesky" | custom-call | tf_op jit(solution)/shard_map/jit(cholesky)/cholesky | solution.py:63
  408.9 4.9 %custom-call.26 = f32[1,64,64]{1,2,0:T(8,128)S(1)} custom-call(f32[1,64,64]{2,1,0:T(8,128)S(1)} %fusion.50), custom_call_target="InvertDiagBlocksLowerTriangular" | custom-call | tf_op jit(solution)/shard_map/jit(_solve_triangular)/triangular_solve | solution.py:11
  415.1 40.1 %all-reduce = (f32[64]{0:T(128)S(1)}, f32[64]{0:T(128)S(1)}) all-reduce(f32[64]{0:T(128)S(1)} %get-tuple-element.44, f32[64]{0:T(128)S(1)} %get-tuple-element.46), channel_id=1, replica_groups=mesh['rows'=16,'panel'=2] {'rows','panel'}, use_global_device_ids=true, to_apply=%region_20.25 | all-reduce | flops 128 | bytes 1024 | tf_op jit(solution)/shard_map/psum | solution.py:69
  455.2 0.7 copy.51
  (91 shorter events, 16.8 us)
Async XLA Ops:
  7.2 51.5 %copy-start = (bf16[1,1,2,16,128,128]{5,4,3,2,1,0:T(8,128)(2,1)S(1)}, bf16[1,1,2,16,128,128]{5,4,3,2,1,0:T(8,128)(2,1)}, u32[]{:S(2)}) copy-start(bf16[1,1,2,16,128,128]{5,4,3,2,1,0:T(8,128)(2,1)} %param.15) | copy-start | bytes 3145732
  7.2 50.3 %copy-start.6 = (s32[1,1,2]{2,1,0:T(1,128)S(1)}, s32[1,1,2]{2,1,0:T(1,128)}, u32[]{:S(2)}) copy-start(s32[1,1,2]{2,1,0:T(1,128)} %param.16) | copy-start | bytes 28
  7.2 56.4 %reduce-scatter.4.cloned.1.call-start = ((), (), s32[]{:S(2)}) async-start(), calls=%async_computation.3 | async-start | bytes 294912 | tf_op jit(solution)/shard_map/reduce_scatter | solution.py:47
  58.6 1.4 copy-start.1
  58.7 1.6 copy-start.4
  58.7 1.6 copy-start.5
  60.0 151.3 %reduce-scatter.6.cloned.1.call-start = ((), (), s32[]{:S(2)}) async-start(), calls=%async_computation.4 | async-start | bytes 294912 | tf_op jit(solution)/shard_map/reduce_scatter | solution.py:47
  206.4 4.9 %copy-start.2 = (f32[3,64,192]{2,1,0:T(8,128)S(1)}, f32[3,64,192]{2,1,0:T(8,128)}, u32[]{:S(2)}) copy-start(f32[3,64,192]{2,1,0:T(8,128)} %param.21) | copy-start | bytes 442372
  207.7 151.5 %reduce-scatter.8.cloned.1.call-start = ((), (), s32[]{:S(2)}) async-start(), calls=%async_computation.5 | async-start | bytes 294912 | tf_op jit(solution)/shard_map/reduce_scatter | solution.py:47
  414.3 43.0 %copy-start.3 = (f32[64,128]{1,0:T(8,128)}, f32[64,128]{1,0:T(8,128)S(1)}, u32[]{:S(2)}) copy-start(f32[64,128]{1,0:T(8,128)S(1)} %fusion.66) | copy-start | bytes 98308
Sparse Core Ops, SparseCore 0:
  60.1 3.4 reduce-scatter.3
  207.9 3.4 reduce-scatter.5
  355.8 3.4 reduce-scatter.7
where the time goes:
time: 465 us; the launch traced here: 464 us
  blocking collectives  381 us (82%)
  other arithmetic  38.8 us (8%)
  between operations  14.3 us (3%)
  matrix products  13.6 us (3%)
  local copies, waits for them, and re-layouts  9.17 us (2%)
  waiting for transfers between devices  6.79 us (1%)
    psum x5, blocking collectives, body(): lax.psum((jnp.dot(rotated, rotated.T, precision=highest), jnp.dot(rotated...  203 us
    all_gather x3, blocking collectives, body(): stacked_all = lax.all_gather(stacked, 'rows', axis=1, tiled=True)  138 us
    psum x1, blocking collectives, body(): lax.psum(jnp.sum(resid_raw * resid_raw, axis=1), ('rows', 'panel'))  40.1 us
    another operation x9, other arithmetic, body(): factor = jnp.linalg.cholesky(gram_sum / node_total)  19.6 us
    another operation x6, other arithmetic, lower_solve(): return jax.scipy.linalg.solve_triangular(factor, values, lower=True)  16.6 us
  transfers between devices with their start and end apart: 3, of which 3 were waited for; matrix products, arithmetic and copies ran while one was open for 1% of the time, Pallas kernels for 0%

commit v1 on v0

--- a/solution.py
+++ b/solution.py
@@ -5,6 +5,12 @@
 
 epsilon = 1e-06
 highest = lax.Precision.HIGHEST
+
+
+def add_all(x, name):
+    parts = lax.all_gather(x, name, axis=0, tiled=False)
+    total = parts.sum(axis=0)
+    return total
 
 
 def lower_solve(factor, values):
@@ -66,7 +72,7 @@
         rayleigh = lower_solve(factor, lower_solve(factor, curve_sum / node_total).T).T
         resid_raw = basis_image - jnp.dot(rayleigh.T, basis, precision=highest)
         search_sq = search_sum / node_total
-        resid_sq = lax.psum(jnp.sum(resid_raw * resid_raw, axis=1), ("rows", "panel")) / node_total
+        resid_sq = add_all(jnp.sum(resid_raw * resid_raw, axis=1), ("rows", "panel")) / node_total
         resid = resid_raw / jnp.sqrt(resid_sq + epsilon)[:, None]
         search = search_raw / jnp.sqrt(search_sq + epsilon)[:, None]
         basis_b = basis.astype(jnp.bfloat16)

time: 465 us -> 467 us (level)
    unnamed x0 -> x1, blocking collectives: none -> 40.3 us
    psum x1 -> x0, blocking collectives: 40.1 us -> none  [body(): lax.psum(jnp.sum(resid_raw * resid_raw, axis=1), ('rows', 'panel'))]
where the time goes in v1:
time: 467 us; the launch traced here: 465 us
  blocking collectives  381 us (82%)
  other arithmetic  38.9 us (8%)
  between operations  14.4 us (3%)
  matrix products  13.6 us (3%)
  local copies, waits for them, and re-layouts  10.2 us (2%)
  waiting for transfers between devices  6.77 us (1%)
    psum x5, blocking collectives, body(): lax.psum((jnp.dot(rotated, rotated.T, precision=highest), jnp.dot(rotated...  204 us
    all_gather x3, blocking collectives, body(): stacked_all = lax.all_gather(stacked, 'rows', axis=1, tiled=True)  138 us
    unnamed x1, blocking collectives  40.3 us
    another operation x9, other arithmetic, body(): factor = jnp.linalg.cholesky(gram_sum / node_total)  19.6 us
    another operation x6, other arithmetic, lower_solve(): return jax.scipy.linalg.solve_triangular(factor, values, lower=True)  16.6 us
  transfers between devices with their start and end apart: 3, of which 3 were waited for; matrix products, arithmetic and copies ran while one was open for 1% of the time, Pallas kernels for 0%

profile of v1, /device:TPU:0, one launch (start us, length us, event | category | flops | bytes accessed | tf_op | source)
XLA Modules:
  0.0 465.3 jit_solution(14981475848559828143)
XLA Ops:
  7.2 0.8 reshape_squeeze.2
  8.1 0.7 constant_dynamic-update-slice_fusion.2
  8.8 0.7 constant_dynamic-update-slice_fusion.1
  9.5 0.7 constant_dynamic-update-slice_fusion
  10.3 47.0 %all_gather.27 = bf16[192,2048]{1,0:T(8,128)(2,1)S(1)} all-gather(bf16[192,128]{1,0:T(8,128)(2,1)S(1)} %constant_dynamic-update-slice_fusion), channel_id=1, replica_groups=mesh['rows'=16,'panel'=2] {'rows'}, dimensions={1}, use_global_device_ids=true | all-gather | bytes 835584 | tf_op jit(solution)/shard_map/all_gather | solution.py:51
  57.6 0.8 gather_fusion
  60.3 1.0 multiply_reduce_fusion.4
  61.5 2.1 reduce-scatter.4.cloned.1.call-done
  63.6 1.1 fusion.30
  64.9 41.0 %all-reduce.8 = (f32[64,64]{0,1:T(8,128)S(1)}, f32[64,64]{0,1:T(8,128)S(1)}) all-reduce(f32[64,64]{0,1:T(8,128)S(1)} %fusion.122, f32[64,64]{0,1:T(8,128)S(1)} %fusion.123), channel_id=1, replica_groups=mesh['rows'=16,'panel'=2] {'rows','panel'}, use_global_device_ids=true, to_apply=%region_0.1 | all-reduce | flops 8192 | bytes 65536 | tf_op jit(solution)/shard_map/psum | solution.py:61
  106.1 5.8 %cholesky.59 = f32[64,64]{1,0:T(8,128)S(1)} custom-call(f32[64,64]{1,0:T(8,128)S(1)} %fusion.95), custom_call_target="Cholesky" | custom-call | tf_op jit(solution)/shard_map/jit(cholesky)/cholesky | solution.py:69
  113.3 4.9 %custom-call.18 = f32[1,64,64]{1,2,0:T(8,128)S(1)} custom-call(f32[1,64,64]{2,1,0:T(8,128)S(1)} %fusion.48), custom_call_target="InvertDiagBlocksLowerTriangular" | custom-call | tf_op jit(solution)/shard_map/jit(_solve_triangular)/triangular_solve | solution.py:17
  119.7 40.1 %all-reduce.7 = (f32[64]{0:T(128)S(1)}, f32[2048]{0:T(1024)S(1)}) all-reduce(f32[64]{0:T(128)S(1)} %get-tuple-element.36, f32[2048]{0:T(1024)S(1)} %dynamic-update-slice.2), channel_id=1, replica_groups=mesh['rows'=16,'panel'=2] {'rows','panel'}, use_global_device_ids=true, to_apply=%region_8.13 | all-reduce | flops 2112 | bytes 16896 | tf_op jit(solution)/shard_map/psum | solution.py:61
  160.3 45.3 %all_gather.30 = bf16[192,2048]{1,0:T(8,128)(2,1)S(1)} all-gather(bf16[192,128]{1,0:T(8,128)(2,1)S(1)} %pad_maximum_fusion), channel_id=1, replica_groups=mesh['rows'=16,'panel'=2] {'rows'}, dimensions={1}, use_global_device_ids=true | all-gather | bytes 835584 | tf_op jit(solution)/shard_map/all_gather | solution.py:51
  205.8 0.9 gather_fusion.1
  208.2 1.0 multiply_reduce_fusion.2
  209.5 2.3 reduce-scatter.6.cloned.1.call-done
  211.8 1.1 fusion.27
  213.1 41.0 %all-reduce.6 = (f32[64,64]{0,1:T(8,128)S(1)}, f32[64,64]{0,1:T(8,128)S(1)}) all-reduce(f32[64,64]{0,1:T(8,128)S(1)} %fusion.124, f32[64,64]{0,1:T(8,128)S(1)} %fusion.125), channel_id=1, replica_groups=mesh['rows'=16,'panel'=2] {'rows','panel'}, use_global_device_ids=true, to_apply=%region_9.14 | all-reduce | flops 8192 | bytes 65536 | tf_op jit(solution)/shard_map/psum | solution.py:61
  254.2 5.8 %cholesky.70 = f32[64,64]{1,0:T(8,128)S(1)} custom-call(f32[64,64]{1,0:T(8,128)S(1)} %fusion.84), custom_call_target="Cholesky" | custom-call | tf_op jit(solution)/shard_map/jit(cholesky)/cholesky | solution.py:69
  261.4 4.9 %custom-call.22 = f32[1,64,64]{1,2,0:T(8,128)S(1)} custom-call(f32[1,64,64]{2,1,0:T(8,128)S(1)} %fusion.49), custom_call_target="InvertDiagBlocksLowerTriangular" | custom-call | tf_op jit(solution)/shard_map/jit(_solve_triangular)/triangular_solve | solution.py:17
  267.9 40.3 %all-reduce.5 = (f32[64]{0:T(128)S(1)}, f32[2048]{0:T(1024)S(1)}) all-reduce(f32[64]{0:T(128)S(1)} %get-tuple-element.40, f32[2048]{0:T(1024)S(1)} %dynamic-update-slice.3), channel_id=1, replica_groups=mesh['rows'=16,'panel'=2] {'rows','panel'}, use_global_device_ids=true, to_apply=%region_15.20 | all-reduce | flops 2112 | bytes 16896 | tf_op jit(solution)/shard_map/psum | solution.py:61
  308.7 45.3 %all_gather.33 = bf16[192,2048]{1,0:T(8,128)(2,1)S(1)} all-gather(bf16[192,128]{1,0:T(8,128)(2,1)S(1)} %pad_maximum_fusion.1), channel_id=1, replica_groups=mesh['rows'=16,'panel'=2] {'rows'}, dimensions={1}, use_global_device_ids=true | all-gather | bytes 835584 | tf_op jit(solution)/shard_map/all_gather | solution.py:51
  354.2 0.9 gather_fusion.2
  356.6 1.0 multiply_reduce_fusion
  357.8 2.4 reduce-scatter.8.cloned.1.call-done
  360.2 1.1 fusion.24
  361.5 41.0 %all-reduce.4 = (f32[64,64]{0,1:T(8,128)S(1)}, f32[64,64]{0,1:T(8,128)S(1)}) all-reduce(f32[64,64]{0,1:T(8,128)S(1)} %fusion.126, f32[64,64]{0,1:T(8,128)S(1)} %fusion.127), channel_id=1, replica_groups=mesh['rows'=16,'panel'=2] {'rows','panel'}, use_global_device_ids=true, to_apply=%region_16.21 | all-reduce | flops 8192 | bytes 65536 | tf_op jit(solution)/shard_map/psum | solution.py:61
  402.6 5.8 %cholesky.81 = f32[64,64]{1,0:T(8,128)S(1)} custom-call(f32[64,64]{1,0:T(8,128)S(1)} %fusion.73), custom_call_target="Cholesky" | custom-call | tf_op jit(solution)/shard_map/jit(cholesky)/cholesky | solution.py:69
  409.8 4.9 %custom-call.26 = f32[1,64,64]{1,2,0:T(8,128)S(1)} custom-call(f32[1,64,64]{2,1,0:T(8,128)S(1)} %fusion.50), custom_call_target="InvertDiagBlocksLowerTriangular" | custom-call | tf_op jit(solution)/shard_map/jit(_solve_triangular)/triangular_solve | solution.py:17
  416.2 40.3 %all-reduce.3 = (f32[2048]{0:T(1024)S(1)}, f32[64]{0:T(128)S(1)}) all-reduce(f32[2048]{0:T(1024)S(1)} %dynamic-update-slice.4, f32[64]{0:T(128)S(1)} %get-tuple-element.50), channel_id=4, replica_groups=mesh['rows'=16,'panel'=2] {'rows','panel'}, use_global_device_ids=true, to_apply=%add.2 | all-reduce | flops 2112 | bytes 16896
  456.6 0.7 copy.67
  (104 shorter events, 18.0 us)
Async XLA Ops:
  7.2 51.5 %copy-start = (bf16[1,1,2,16,128,128]{5,4,3,2,1,0:T(8,128)(2,1)S(1)}, bf16[1,1,2,16,128,128]{5,4,3,2,1,0:T(8,128)(2,1)}, u32[]{:S(2)}) copy-start(bf16[1,1,2,16,128,128]{5,4,3,2,1,0:T(8,128)(2,1)} %param.15) | copy-start | bytes 3145732
  7.2 50.3 %copy-start.6 = (s32[1,1,2]{2,1,0:T(1,128)S(1)}, s32[1,1,2]{2,1,0:T(1,128)}, u32[]{:S(2)}) copy-start(s32[1,1,2]{2,1,0:T(1,128)} %param.16) | copy-start | bytes 28
  7.2 56.4 %reduce-scatter.4.cloned.1.call-start = ((), (), s32[]{:S(2)}) async-start(), calls=%async_computation.3 | async-start | bytes 294912 | tf_op jit(solution)/shard_map/reduce_scatter | solution.py:53
  58.6 1.4 copy-start.1
  58.7 1.6 copy-start.4
  58.7 1.6 copy-start.5
  60.0 151.8 %reduce-scatter.6.cloned.1.call-start = ((), (), s32[]{:S(2)}) async-start(), calls=%async_computation.4 | async-start | bytes 294912 | tf_op jit(solution)/shard_map/reduce_scatter | solution.py:53
  206.8 4.9 %copy-start.2 = (f32[3,64,192]{2,1,0:T(8,128)S(1)}, f32[3,64,192]{2,1,0:T(8,128)}, u32[]{:S(2)}) copy-start(f32[3,64,192]{2,1,0:T(8,128)} %param.21) | copy-start | bytes 442372
  208.2 152.0 %reduce-scatter.8.cloned.1.call-start = ((), (), s32[]{:S(2)}) async-start(), calls=%async_computation.5 | async-start | bytes 294912 | tf_op jit(solution)/shard_map/reduce_scatter | solution.py:53
  415.2 43.5 %copy-start.3 = (f32[64,128]{1,0:T(8,128)}, f32[64,128]{1,0:T(8,128)S(1)}, u32[]{:S(2)}) copy-start(f32[64,128]{1,0:T(8,128)S(1)} %fusion.66) | copy-start | bytes 98308
Sparse Core Ops, SparseCore 0:
  60.1 3.4 reduce-scatter.3
  208.3 3.4 reduce-scatter.5
  356.7 3.4 reduce-scatter.7
